TPU v7x, 128 devices: a whole 4x4x4 slice. The times are simulated.
128 devices in a mesh: dp: 32 (over y, z, core), tensor: 4 (over x).
Axes of the slice: x: 4, y: 4, z: 4, core: 2. Of those that a mesh axis runs over, the one named last changes fastest.
Arguments:
- tokens: bfloat16 [16384, 4096], P('dp', 'tensor'), may hold values from -6 to 6
- grad_out: bfloat16 [16384, 4096], P('dp'), may hold values from -3 to 3
- gate_pre: bfloat16 [16384, 14336], P('dp', 'tensor'), may hold values from -9 to 9
- up_value: bfloat16 [16384, 14336], P('dp', 'tensor'), may hold values from -6 to 6
- down_weight: bfloat16 [14336, 4096], P('tensor', 'dp'), may hold values from -0.09375 to 0.09375
- in_proj: bfloat16 [128, 4096], P(None, 'tensor'), may hold values from -0.09375 to 0.09375
- out_proj: bfloat16 [128, 14336], P(None, 'tensor'), may hold values from -0.046875 to 0.046875
- test_matrix: bfloat16 [16384, 128], replicated, may hold values from -0.046875 to 0.046875
Outputs:
- factor: float32 [16384, 128], P(('dp', 'tensor'))
All inputs are finite; a program needn't handle non-finite values.
Results may differ from a plain program's by a relative error of at most 0.0065.
The roundings to bfloat16 on the way count: a program that leaves them out, or rounds other values in their place, can miss the bound.
Values may be sent and summed in bfloat16 or wider, within the bound.
A program may use at most 128 MiB of HBM per device.

v0:
```python
import jax
import jax.numpy as jnp
from jax import lax
from jax.sharding import PartitionSpec as P

SEQ_LEN = 128


shift_scale = 0.1
tiny_value = 1e-06


def local(tokens, grad_out, gate_pre, up_value, down_weight, in_proj, out_proj, test_matrix):
    rows = grad_out.shape[0]
    hidden_grad = lax.dot_general(
        grad_out,
        lax.all_gather(down_weight, "dp", axis=1, tiled=True),
        (((1,), (1,)), ((), ())),
        preferred_element_type=jnp.float32,
    )
    gate_wide = gate_pre.astype(jnp.float32)
    logistic = jax.nn.sigmoid(gate_wide)
    gate_grad = (
        hidden_grad * up_value.astype(jnp.float32) * logistic * (1.0 + gate_wide * (1.0 - logistic))
    ).astype(jnp.bfloat16)
    act_part = lax.dot_general(
        tokens, in_proj, (((1,), (1,)), ((), ())), preferred_element_type=jnp.float32
    )
    out_part = lax.dot_general(
        gate_grad, out_proj, (((1,), (1,)), ((), ())), preferred_element_type=jnp.float32
    )
    act_sum, out_sum = lax.psum((act_part, out_part), "tensor")
    pdim = in_proj.shape[0]
    rank_cols = test_matrix.shape[1]
    seqs_here = rows // SEQ_LEN
    act_seq = act_sum.astype(jnp.bfloat16).reshape(seqs_here, SEQ_LEN, pdim)
    out_seq = out_sum.astype(jnp.bfloat16).reshape(seqs_here, SEQ_LEN, pdim)
    proj_grad = (
        jnp.einsum("slp,slq->spq", act_seq, out_seq, preferred_element_type=jnp.float32)
        .astype(jnp.bfloat16)
        .reshape(seqs_here, pdim * pdim)
    )
    coeff = jnp.dot(proj_grad, test_matrix, preferred_element_type=jnp.float32).astype(jnp.bfloat16)
    dp_count = lax.axis_size("dp")
    tp_count = lax.axis_size("tensor")
    tp_index = lax.axis_index("tensor")
    dp_index = lax.axis_index("dp")
    width = pdim * pdim // (dp_count * tp_count)
    picked = lax.dynamic_slice_in_dim(
        proj_grad.reshape(seqs_here, dp_count, tp_count, width), tp_index, 1, 2
    ).reshape(seqs_here, dp_count * width)
    omega_wide = test_matrix.astype(jnp.float32)
    omega_picked = lax.dynamic_slice_in_dim(
        omega_wide.reshape(dp_count, tp_count, width, rank_cols), tp_index, 1, 1
    ).reshape(dp_count * width, rank_cols)
    omega_own = lax.dynamic_slice_in_dim(omega_picked, dp_index * width, width, 0)
    sketch_part = lax.dot_general(
        picked, coeff, (((0,), (0,)), ((), ())), preferred_element_type=jnp.float32
    )
    gram = lax.dot_general(
        test_matrix, test_matrix, (((0,), (0,)), ((), ())), preferred_element_type=jnp.float32
    )
    omega_sq = jnp.trace(gram)
    summed = lax.psum(sketch_part, "dp")
    core_local = lax.dot_general(
        omega_picked, summed, (((0,), (0,)), ((), ())), precision=lax.Precision.HIGHEST
    )
    square_sum, core_sketch = lax.psum((jnp.sum(summed * summed), core_local), "tensor")
    own_rows = lax.dynamic_slice_in_dim(summed, dp_index * width, width, 0)
    shift = shift_scale * jnp.sqrt(square_sum / (omega_sq + tiny_value))
    core = core_sketch + shift * gram
    core = 0.5 * (core + core.T)
    lower = jnp.linalg.cholesky(core)
    shifted = own_rows + shift * omega_own
    factor = jax.scipy.linalg.solve_triangular(lower, shifted.T, lower=True).T
    return factor


def solution(mesh):
    in_specs = (
        P("dp", "tensor"),
        P("dp", None),
        P("dp", "tensor"),
        P("dp", "tensor"),
        P("tensor", "dp"),
        P(None, "tensor"),
        P(None, "tensor"),
        P(),
    )
    out_specs = P(("dp", "tensor"), None)
    return jax.shard_map(local, mesh=mesh, in_specs=in_specs, out_specs=out_specs, check_vma=False)
```

profile of v0, /device:TPU:1, one launch (start us, length us, event | category | flops | bytes accessed | tf_op | source)
XLA Modules:
  0.0 360.9 jit_solution(9847140538251873871)
XLA Ops:
  6.5 0.0 copy-start
  6.5 0.0 all-gather.2.cloned.1.call-start
  6.5 0.7 all-gather.2.cloned.1.call-update
  7.3 0.0 all-reduce.5.cloned.1.call-start
  7.3 0.5 copy-done
  7.8 1.4 fusion.24
  9.2 117.4 %all-gather.2.cloned.1.call-done = bf16[3584,4096]{1,0:T(8,128)(2,1)} async-done(((bf16[3584,128]{1,0:T(8,128)(2,1)}), bf16[3584,4096]{1,0:T(8,128)(2,1)}) %all-gather.2.cloned.1.call-update) | async-done | bytes 29360144 | tf_op jit(solution)/shard_map/all_gather | solution.py:17
  126.5 24.7 %fusion.25 = f32[512,128]{1,0:T(8,128)S(1)} fusion(bf16[128,3584]{1,0:T(8,128)(2,1)} %param.14, bf16[512,3584]{1,0:T(8,128)(2,1)} %param.10, bf16[512,3584]{1,0:T(8,128)(2,1)} %param.11, bf16[512,4096]{1,0:T(8,128)(2,1)} %param.9, bf16[3584,4096]{1,0:T(8,128)(2,1)} %all-gather.2.cloned.1.call-done), kind=kOutput, calls=%fused_computation.40 | convolution fusion | flops 15524167680 | bytes 42074112 | tf_op jit(solution)/shard_map/dot_general | solution.py:29
  151.2 19.1 %all-reduce.8 = (bf16[512,128]{1,0:T(8,128)(2,1)S(1)}, bf16[512,128]{1,0:T(8,128)(2,1)S(1)}) all-reduce(f32[512,128]{1,0:T(8,128)S(1)} %fusion.24, f32[512,128]{1,0:T(8,128)S(1)} %fusion.25), channel_id=1, replica_groups=mesh['dp'=32,'tensor'=4] {'tensor'}, use_global_device_ids=true, to_apply=%region_0.0 | all-reduce | flops 131072 | bytes 786432 | tf_op jit(solution)/shard_map/psum | solution.py:32
  170.3 0.2 convolution_convert_fusion
  170.5 0.2 dynamic-slice_reduce_fusion
  170.8 4.7 %fusion.6 = f32[4096,128]{0,1:T(8,128)} fusion(bf16[16384,128]{1,0:T(8,128)(2,1)} %param.15, bf16[1,4,128,128]{3,2,1,0:T(8,128)(2,1)S(1)} %bitcast.60, bf16[1,4,32,128]{3,2,1,0:T(8,128)(2,1)S(1)} %bitcast.61), kind=kOutput, calls=%fused_computation.12 | convolution fusion | flops 20972032 | bytes 6455296 | tf_op jit(solution)/shard_map/dot_general | solution.py:57
  175.4 0.0 all-reduce.5.cloned.1.call-update
  175.4 0.2 all-reduce.7.cloned.1.call-start
  175.7 5.4 %select_reduce_fusion.1 = (f32[]{:T(128)}, f32[128,128]{1,0:T(8,128)S(1)}) fusion(bf16[16384,128]{1,0:T(8,128)(2,1)} %param.15), kind=kOutput, calls=%fused_computation.29 | convolution fusion | flops 536920064 | bytes 4259844 | tf_op jit(solution)/shard_map/dot_general | solution.py:60
  181.1 0.1 copy.21
  181.1 1.3 constant_dynamic-slice_fusion
  182.5 1.0 copy.28
  183.4 0.3 reshape.38
  183.7 2.9 copy.42
  186.7 99.8 %all-reduce.5.cloned.1.call-done = f32[4096,128]{0,1:T(8,128)} async-done(((f32[4096,128]{0,1:T(8,128)}), f32[4096,128]{0,1:T(8,128)}) %all-reduce.5.cloned.1.call-update) | async-done | bytes 2097168 | tf_op jit(solution)/shard_map/psum | solution.py:64
  286.5 3.3 fusion.26
  289.8 0.0 all-reduce.7.cloned.1.call-update
  289.8 2.7 multiply_reduce_fusion
  293.2 9.0 %psum.38 = f32[]{:T(128)} all-reduce(f32[]{:T(128)} %multiply_reduce_fusion), channel_id=1, replica_groups=mesh['dp'=32,'tensor'=4] {'tensor'}, use_global_device_ids=true, to_apply=%region_4.5 | all-reduce | flops 1 | bytes 8 | tf_op jit(solution)/shard_map/psum | solution.py:68
  302.8 25.9 %all-reduce.7.cloned.1.call-done = f32[128,128]{0,1:T(8,128)} async-done(((f32[128,128]{0,1:T(8,128)}), f32[128,128]{0,1:T(8,128)}) %all-reduce.7.cloned.1.call-update) | async-done | bytes 65552 | tf_op jit(solution)/shard_map/psum | solution.py:68
  328.7 0.8 multiply_add_fusion
  329.5 0.1 copy.22
  329.6 0.1 copy.23
  329.7 11.7 %cholesky.13 = f32[128,128]{1,0:T(8,128)S(1)} custom-call(f32[128,128]{1,0:T(8,128)S(1)} %fusion.14), custom_call_target="Cholesky" | custom-call | tf_op jit(solution)/shard_map/jit(cholesky)/cholesky | solution.py:73
  341.5 0.6 compare_reduce_fusion
  342.1 0.7 fusion.11
  342.8 9.8 %custom-call.7 = f32[1,128,128]{1,2,0:T(8,128)S(1)} custom-call(f32[1,128,128]{2,1,0:T(8,128)S(1)} %fusion.11), custom_call_target="InvertDiagBlocksLowerTriangular" | custom-call | tf_op jit(solution)/shard_map/jit(_solve_triangular)/triangular_solve | solution.py:75
  352.6 1.8 fusion.12
  (3 shorter events, 0.1 us)
Async XLA Ops:
  6.5 1.2 copy-start
  6.5 120.0 %all-gather.2.cloned.1.call-start = ((), (), s32[]{:S(2)}) async-start(), calls=%async_computation | async-start | bytes 30277632 | tf_op jit(solution)/shard_map/all_gather | solution.py:17
  7.3 279.2 %all-reduce.5.cloned.1.call-start = ((), (), s32[]{:S(2)}) async-start(), calls=%async_computation.1 | async-start | bytes 4194304 | tf_op jit(solution)/shard_map/psum | solution.py:64
  175.4 153.2 %all-reduce.7.cloned.1.call-start = ((), (), s32[]{:S(2)}) async-start(), calls=%async_computation.2 | async-start | bytes 131072 | tf_op jit(solution)/shard_map/psum | solution.py:68
Sparse Core Ops, SparseCore 0:
  9.5 116.9 all-gather.1
  175.6 110.8 all-reduce.4
  290.0 38.6 all-reduce.6
where the time goes:
time: 363 us; the launch traced here: 361 us
  waiting for transfers between devices  244 us (67%)
  matrix products  41.5 us (11%)
  blocking collectives  28.1 us (8%)
  other arithmetic  26.7 us (7%)
  between operations  14.4 us (4%)
  local copies, waits for them, and re-layouts  6.14 us (2%)
    all_gather x1, waiting for transfers between devices, local(): lax.all_gather(down_weight, 'dp', axis=1, tiled=True)  117 us
    psum x1, waiting for transfers between devices, local(): summed = lax.psum(sketch_part, 'dp')  99.8 us
    psum x1, waiting for transfers between devices, local(): lax.psum((jnp.sum(summed * summed), core_local), 'tensor')  25.9 us
    dot_general x1, matrix products, local(): lax.dot_general(gate_grad, out_proj, (((1,), (1,)), ((), ())), preferred_...  24.7 us
    psum x1, blocking collectives, local(): act_sum, out_sum = lax.psum((act_part, out_part), 'tensor')  19.1 us
    another operation x3, other arithmetic, local(): lower = jnp.linalg.cholesky(core)  12.4 us
    another operation x2, other arithmetic, local(): factor = jax.scipy.linalg.solve_triangular(lower, shifted.T, lower=True).T  10.5 us
    psum x1, blocking collectives, local(): lax.psum((jnp.sum(summed * summed), core_local), 'tensor')  9.02 us
  transfers between devices with their start and end apart: 3, of which 3 were waited for; matrix products, arithmetic and copies ran while one was open for 4% of the time, Pallas kernels for 0%

commit v1 on v0

v1 whole, which is shorter than its diff:
```python
import functools

import jax
import jax.numpy as jnp
from jax import lax
from jax.experimental import pallas as pl
from jax.experimental.pallas import tpu as pltpu
from jax.sharding import PartitionSpec as P

MESH = pl.DeviceIdType.MESH
shift_scale = 0.1
tiny_value = 1e-06

ORDER = [
    (0, 0), (3, 0), (1, 0), (0, 3), (0, 1), (2, 0), (3, 3), (3, 1),
    (1, 3), (1, 1), (0, 2), (2, 3), (2, 1), (3, 2), (1, 2), (2, 2),
]
SLOT = {home: k for k, home in enumerate(ORDER)}
ROWS = {(0, 0): (0, 512), (0, 1): (512, 512), (1, 0): (1024, 384), (1, 1): (1408, 384)}
UP, UM, VP, VM = 0, 1, 2, 3
NSEND = 60


def table(k, values):
    total = k * 0
    for j, v in enumerate(values):
        if v:
            total = total + (k == j).astype(jnp.int32) * v
    return total


def nt(a, b):
    return lax.dot_general(a, b, (((1,), (1,)), ((), ())), preferred_element_type=jnp.float32)


def tn(a, b, **kw):
    return lax.dot_general(a, b, (((0,), (0,)), ((), ())), preferred_element_type=jnp.float32, **kw)


def kernel(
    tok_h, go_h, gp_h, up_h, dw_h, ip_h, op_h, tm_h,
    y_o, a_o, gram_o, nr_o, om_o,
    w_s, g_s, gp_s, up_s, acc_s, m_s, tk_s, ip_s, op_s, tm_s,
    oacc_s, sb_s, pb_s, oa_s, xb_s, xr_s, ap_s, ar_s,
    p32_s, pr_s, cs_s, cr_s, ns_s, nr_s,
    lsem, psend, precv, ssem, rsem, sbsend, sbrecv, xsend, xrecv, asend, arecv, tsend, trecv,
):
    d = lax.axis_index("dp")
    t = lax.axis_index("tensor")
    c = lax.rem(d, 2)
    z = lax.rem(lax.div(d, 2), 4)
    y = lax.div(d, 8)
    u = y * (1 - c) + z * c
    v = z * (1 - c) + y * c
    me = d * 4 + t

    def chip(uu, vv):
        return uu * (4 - 3 * c) + vv * (1 + 3 * c)

    def mod4(a):
        return lax.rem(a + 8, 4)

    partner = (d + 1 - 2 * c, t)
    dirs = [
        (chip(mod4(u + 1), v) * 2 + c, t),
        (chip(mod4(u - 1), v) * 2 + c, t),
        (chip(u, mod4(v + 1)) * 2 + c, t),
        (chip(u, mod4(v - 1)) * 2 + c, t),
    ]
    xdev = [None] + [(d, mod4(t + j)) for j in (1, 2, 3)]

    half = pl.multiple_of(c * 1792, 256)
    other = pl.multiple_of((1 - c) * 1792, 256)
    mine = pl.ds(pl.multiple_of(c * 512, 512), 512)
    lanes = pl.ds(pl.multiple_of(c * 128, 128), 128)

    def local(i, src, dst):
        return pltpu.make_async_copy(src, dst, lsem.at[i])

    def locals_(i):
        if i == 0:
            return local(0, dw_h.at[pl.ds(half, 1024)], w_s.at[0, pl.ds(0, 1024), lanes])
        if i == 1:
            return local(1, dw_h.at[pl.ds(half + 1024, 768)], w_s.at[0, pl.ds(1024, 768), lanes])
        src, dst = [
            (go_h, g_s.at[mine]),
            (tok_h, tk_s),
            (ip_h, ip_s),
            (op_h.at[:, pl.ds(half, 1792)], op_s),
            (gp_h.at[:, pl.ds(half, 1792)], gp_s.at[mine]),
            (up_h.at[:, pl.ds(half, 1792)], up_s.at[mine]),
            (tm_h, tm_s),
        ][i - 2]
        return local(i, src, dst)

    for i in range(5):
        locals_(i).start()

    barrier = pltpu.get_barrier_semaphore()
    greeted = [partner] + dirs + xdev[1:]
    for dev in greeted:
        pl.semaphore_signal(barrier, 1, device_id=dev, device_id_type=MESH)
    pl.semaphore_wait(barrier, len(greeted))

    def remote(src, dst, ss, rs, dev):
        return pltpu.make_async_remote_copy(
            src_ref=src, dst_ref=dst, send_sem=ss, recv_sem=rs, device_id=dev, device_id_type=MESH
        )

    def partner_copies(i):
        src, dst = [
            lambda: (dw_h.at[pl.ds(other, 1024)], w_s.at[0, pl.ds(0, 1024), lanes]),
            lambda: (dw_h.at[pl.ds(other + 1024, 768)], w_s.at[0, pl.ds(1024, 768), lanes]),
            lambda: (go_h, g_s.at[mine]),
            lambda: (gp_h.at[:, pl.ds(other, 1792)], gp_s.at[mine]),
            lambda: (up_h.at[:, pl.ds(other, 1792)], up_s.at[mine]),
        ][i]()
        return remote(src, dst, psend.at[i], precv.at[i], partner)

    partner_copies(0).start()
    partner_copies(1).start()
    partner_copies(2).start()

    sends = []

    def send(dirn, src, dst, w, h):
        r0, rn = ROWS[(w, h)]
        rows = pl.ds(r0, rn)
        remote(
            w_s.at[SLOT[src], rows], w_s.at[SLOT[dst], rows],
            ssem.at[len(sends)], rsem.at[SLOT[dst], 2 * w + h], dirs[dirn],
        ).start()
        sends.append((r0, rn))

    def landed(home, w, h):
        r0, rn = ROWS[(w, h)]
        ref = w_s.at[SLOT[home], pl.ds(r0, rn)]
        remote(ref, ref, ssem.at[0], rsem.at[SLOT[home], 2 * w + h], dirs[0]).wait_recv()

    def event(home, w, h):
        du, dv = home
        landed(home, w, h)
        if dv == 0:
            if du == 3 and h == 0:
                send(UP, home, (2, 0), w, h)
            if du == 1 and h == 1:
                send(UM, home, (2, 0), w, h)
            send(VP, home, (du, 3), w, h)
            send(VM, home, (du, 1), w, h)
        elif dv == 3 and h == 0:
            send(VP, home, (du, 2), w, h)
        elif dv == 1 and h == 1:
            send(VM, home, (du, 2), w, h)

    def own_u(w):
        for k in range(2):
            send(UP, (0, 0), (3, 0), w, k)
            send(UM, (0, 0), (1, 0), w, 1 - k)

    def own_v(w):
        for k in range(2):
            send(VP, (0, 0), (0, 3), w, k)
            send(VM, (0, 0), (0, 1), w, 1 - k)

    locals_(0).wait()
    partner_copies(0).wait_recv()
    own_u(0)
    own_v(0)
    for i in range(5, 9):
        locals_(i).start()
    partner_copies(3).start()
    partner_copies(4).start()

    for n in range(7):
        acc_s[n] = jnp.zeros((1024, 256), jnp.float32)
    locals_(3).wait()
    locals_(4).wait()

    def act_part(j, carry):
        k = mod4(t + j)
        ap_s[j] = nt(tk_s[pl.ds(pl.multiple_of(k * 128, 128), 128), :], ip_s[...])
        return carry

    lax.fori_loop(0, 4, act_part, 0)

    def act_copies(j):
        return remote(ap_s.at[j], ar_s.at[j], asend.at[j], arecv.at[j], xdev[j])

    for j in (2, 1, 3):
        act_copies(j).start()

    def first_events(w):
        event((3, 0), w, 0)
        event((1, 0), w, 1)
        event((3, 0), w, 1)
        event((1, 0), w, 0)

    def pair_events(du, w):
        event((du, 3), w, 0)
        event((du, 1), w, 1)
        event((du, 3), w, 1)
        event((du, 1), w, 0)

    def both(home, w):
        event(home, w, 0)
        event(home, w, 1)

    first_events(0)
    locals_(2).wait()
    partner_copies(2).wait_recv()

    def gate(rows, n):
        cols = pl.ds(n * 256, 256)
        g = gp_s[rows, cols].astype(jnp.float32)
        s = 1.0 / (1.0 + jnp.exp(-g))
        return up_s[rows, cols].astype(jnp.float32) * s * (1.0 + g * (1.0 - s))

    def gate_first():
        def tile(i, carry):
            rows = pl.ds(pl.multiple_of(i * 128, 128), 128)
            total = jnp.zeros((128, 128), jnp.float32)
            for n in range(4):
                gg = (acc_s[n, rows, :] * gate(rows, n)).astype(jnp.bfloat16)
                total = total + nt(gg, op_s[:, n * 256 : (n + 1) * 256])
            oacc_s[i] = total
            return carry

        lax.fori_loop(0, 8, tile, 0)

    def gate_ahead():
        def tile(i, carry):
            rows = pl.ds(pl.multiple_of(i * 128, 128), 128)
            for n in range(3):
                m_s[rows, n * 256 : (n + 1) * 256] = gate(rows, n + 4)
            return carry

        lax.fori_loop(0, 8, tile, 0)

    def gram():
        def part(i, total):
            x = tm_s[pl.ds(pl.multiple_of(i * 1024, 1024), 1024), :]
            return total + tn(x, x)

        gram_o[...] = lax.fori_loop(0, 16, part, jnp.zeros((128, 128), jnp.float32))

    def at(step):
        w, k = divmod(step, 16)
        if k == 0 and w == 1:
            pass
        if k == 3:
            pair_events(0, w)
        if k == 5:
            both((2, 0), w)
            if w == 0:
                locals_(1).wait()
                partner_copies(1).wait_recv()
                own_u(1)
        if k == 6:
            pair_events(3, w)
        if k == 8:
            pair_events(1, w)
        if k == 10:
            pair_events(2, w)
            if w == 0:
                own_v(1)
            both((0, 2), w)
        if k == 13:
            both((3, 2), w)
            if w == 0:
                first_events(1)
        if k == 14:
            both((1, 2), w)
        if k == 15:
            both((2, 2), w)
        if step == 20:
            for i in range(5, 8):
                locals_(i).wait()
            partner_copies(3).wait_recv()
            partner_copies(4).wait_recv()
            gate_first()
        if step == 23:
            gate_ahead()
        if step == 25:
            locals_(8).wait()
            gram()

    def step_body(e, carry):
        for step in range(32):
            if step in (3, 5, 6, 8, 10, 13, 14, 15, 19, 20, 21, 22, 23, 24, 25, 26, 29, 30, 31):
                pl.when(e == step)(functools.partial(at, step))
        w = lax.div(e, 16)
        k = lax.rem(e, 16)
        du = table(k, [h[0] for h in ORDER])
        dv = table(k, [h[1] for h in ORDER])
        q = chip(lax.rem(u + du, 4), lax.rem(v + dv, 4))
        cols = pl.ds(pl.multiple_of(q * 256, 256), 256)

        def part(n, carry):
            m = w * 4 + n
            b = w_s[k, pl.ds(pl.multiple_of(m * 256, 256), 256), :]
            acc_s[m] += nt(g_s[:, cols], b)
            return carry

        lax.fori_loop(0, 4 - w, part, 0)
        return carry

    lax.fori_loop(0, 32, step_body, 0)

    def pb_copy(j):
        return remote(sb_s.at[j], pb_s.at[j], sbsend.at[j], sbrecv.at[j], partner)

    def x_copies(j):
        return remote(xb_s.at[j], xr_s.at[j], xsend.at[j], xrecv.at[j], xdev[j])

    def combine(j):
        pb_copy(j).wait_recv()
        xb_s[j] = oa_s[j] + pb_s[j]
        if j:
            x_copies(j).start()

    def tail(i, carry):
        j = table(lax.div(i, 2), [2, 1, 3, 0])
        own = lax.rem(i, 2)
        core = own * c + (1 - own) * (1 - c)
        k = core * 4 + lax.rem(t + j, 4)
        rows = pl.ds(pl.multiple_of(k * 128, 128), 128)
        total = oacc_s[k]
        for n in range(3):
            gg = (acc_s[n + 4, rows, :] * m_s[rows, n * 256 : (n + 1) * 256]).astype(jnp.bfloat16)
            total = total + nt(gg, op_s[:, (n + 4) * 256 : (n + 5) * 256])

        @pl.when(own == 0)
        def _():
            sb_s[j] = total
            pb_copy(j).start()

        @pl.when(own == 1)
        def _():
            oa_s[j] = total

        for step, jj in ((3, 2), (5, 1), (7, 3)):
            pl.when(i == step)(functools.partial(combine, jj))
        return carry

    lax.fori_loop(0, 8, tail, 0)
    combine(0)
    for j in (1, 2, 3):
        act_copies(j).wait_recv()
    act = (ap_s[0] + ar_s[1] + ar_s[2] + ar_s[3]).astype(jnp.bfloat16)
    for j in (1, 2, 3):
        x_copies(j).wait_recv()
    out = (xb_s[0] + xr_s[1] + xr_s[2] + xr_s[3]).astype(jnp.bfloat16)

    proj = tn(act, out).astype(jnp.bfloat16).astype(jnp.float32)
    p32_s[...] = proj[:, None, :]

    def everyone(copy_to):
        def body(r, carry):
            k = lax.rem(me + r, 128)
            copy_to(k, (lax.div(k, 4), lax.rem(k, 4))).start()
            return carry

        lax.fori_loop(1, 128, body, 0, unroll=4)

    everyone(lambda k, dev: remote(p32_s.at[k], pr_s.at[me], tsend.at[0], trecv.at[0], dev))
    pr_s[me] = p32_s[me]

    def coeff_part(i, totals):
        out = []
        for b in range(8):
            row = p32_s[i * 8 + b].astype(jnp.bfloat16)
            rows = pl.ds(pl.multiple_of(i * 1024 + b * 128, 128), 128)
            out.append(
                totals[b]
                + lax.dot_general(row, tm_s[rows, :], (((1,), (0,)), ((), ())), preferred_element_type=jnp.float32)
            )
        return tuple(out)

    totals = lax.fori_loop(0, 16, coeff_part, tuple(jnp.zeros((1, 128), jnp.float32) for _ in range(8)))
    coeff = ((totals[0] + totals[1]) + (totals[2] + totals[3])) + ((totals[4] + totals[5]) + (totals[6] + totals[7]))
    cs_s[...] = coeff
    everyone(lambda k, dev: remote(cs_s, cr_s.at[me], tsend.at[1], trecv.at[1], dev))
    cr_s[me] = coeff
    om_o[...] = tm_s[pl.ds(pl.multiple_of(me * 128, 128), 128), :].astype(jnp.float32)

    def drain(i, ref):
        return remote(ref.at[pl.ds(0, 127)], ref.at[pl.ds(0, 127)], tsend.at[i], trecv.at[i], partner)

    drain(0, pr_s).wait_recv()
    drain(1, cr_s).wait_recv()
    wide = cr_s[:, 0, :]
    narrow = wide.astype(jnp.bfloat16)
    sketch = tn(pr_s[:, 0, :].astype(jnp.bfloat16), narrow)
    squares = jnp.sum(sketch * sketch, axis=0, keepdims=True)
    ns_s[...] = squares
    everyone(lambda k, dev: remote(ns_s, nr_s.at[me], tsend.at[2], trecv.at[2], dev))
    nr_s[me] = squares
    y_o[...] = sketch
    a_o[...] = tn(wide, narrow.astype(jnp.float32), precision=lax.Precision.HIGHEST)

    for i, (r0, rn) in enumerate(sends):
        ref = w_s.at[0, pl.ds(r0, rn)]
        remote(ref, ref, ssem.at[i], rsem.at[0, 0], dirs[0]).wait_send()
    for i in range(5):
        partner_copies(i).wait_send()
    for j in (1, 2, 3):
        act_copies(j).wait_send()
        x_copies(j).wait_send()
    for j in range(4):
        pb_copy(j).wait_send()
    drain(0, pr_s).wait_send()
    drain(1, cr_s).wait_send()
    drain(2, nr_s).wait_recv()
    drain(2, nr_s).wait_send()
    nr_o[...] = jnp.sum(nr_s[:, 0, :], axis=0, keepdims=True)


def local(tokens, grad_out, gate_pre, up_value, down_weight, in_proj, out_proj, test_matrix):
    f32, bf16 = jnp.float32, jnp.bfloat16
    square = jax.ShapeDtypeStruct((128, 128), f32)
    vmem = pltpu.VMEM
    dma = pltpu.SemaphoreType.DMA
    sketch, core_sketch, gram, squares, omega_own = pl.pallas_call(
        kernel,
        out_shape=(square, square, square, jax.ShapeDtypeStruct((1, 128), f32), square),
        in_specs=[pl.BlockSpec(memory_space=pl.ANY)] * 8,
        out_specs=(pl.BlockSpec(memory_space=vmem),) * 5,
        scratch_shapes=[
            vmem((16, 1792, 256), bf16), vmem((1024, 4096), bf16), vmem((1024, 1792), bf16), vmem((1024, 1792), bf16),
            vmem((7, 1024, 256), f32), vmem((1024, 768), f32), vmem((512, 1024), bf16), vmem((128, 1024), bf16),
            vmem((128, 1792), bf16), vmem((16384, 128), bf16),
            vmem((8, 128, 128), f32), vmem((4, 128, 128), f32), vmem((4, 128, 128), f32), vmem((4, 128, 128), f32),
            vmem((4, 128, 128), f32), vmem((4, 128, 128), f32), vmem((4, 128, 128), f32), vmem((4, 128, 128), f32),
            vmem((128, 1, 128), f32), vmem((128, 1, 128), f32), vmem((1, 128), f32), vmem((128, 1, 128), f32),
            vmem((1, 128), f32), vmem((128, 1, 128), f32),
            dma((9,)), dma((5,)), dma((5,)), dma((NSEND,)), dma((16, 4)), dma((4,)), dma((4,)), dma((4,)), dma((4,)),
            dma((4,)), dma((4,)), dma((3,)), dma((3,)),
        ],
        compiler_params=pltpu.CompilerParams(
            collective_id=1, has_side_effects=True, vmem_limit_bytes=60 * 1024 * 1024
        ),
        name="gather_project_sketch",
    )(tokens, grad_out, gate_pre, up_value, down_weight, in_proj, out_proj, test_matrix)
    shift = shift_scale * jnp.sqrt(jnp.sum(squares) / (jnp.trace(gram) + tiny_value))
    core = core_sketch + shift * gram
    core = 0.5 * (core + core.T)
    lower = jnp.linalg.cholesky(core)
    shifted = sketch + shift * omega_own
    return jax.scipy.linalg.solve_triangular(lower, shifted.T, lower=True).T


def solution(mesh):
    in_specs = (
        P("dp", "tensor"),
        P("dp", None),
        P("dp", "tensor"),
        P("dp", "tensor"),
        P("tensor", "dp"),
        P(None, "tensor"),
        P(None, "tensor"),
        P(),
    )
    out_specs = P(("dp", "tensor"), None)
    return jax.shard_map(local, mesh=mesh, in_specs=in_specs, out_specs=out_specs, check_vma=False)
```

time: 363 us -> 150 us (0.41)
  waiting for transfers between devices: 244 us -> 0 us
  Pallas kernels: 0 us -> 117 us
  matrix products: 41.5 us -> 0.92 us
  blocking collectives: 28.1 us -> 0 us
  between operations: 14.4 us -> 1.45 us
    psum x2 -> x0, waiting for transfers between devices: 126 us -> none  [the longest x1 99.8 us: local(): summed = lax.psum(sketch_part, 'dp')]
    pallas_call x0 -> x1, Pallas kernels: none -> 117 us  [local(): pl.pallas_call(kernel, out_shape=(square, square, square, jax.ShapeDtypeS...]
    all_gather x1 -> x0, waiting for transfers between devices: 117 us -> none  [local(): lax.all_gather(down_weight, 'dp', axis=1, tiled=True)]
    dot_general x6 -> x0, matrix products: 39.7 us -> none  [the longest x1 24.7 us: local(): lax.dot_general(gate_grad, out_proj, (((1,), (1,)), ((), ())), preferred_...]
    psum x2 -> x0, blocking collectives: 28.1 us -> none  [the longest x1 19.1 us: local(): act_sum, out_sum = lax.psum((act_part, out_part), 'tensor')]
    unnamed x4 -> x0, local copies, waits for them, and re-layouts: 4.36 us -> none
    pallas_call x0 -> x4, local copies, waits for them, and re-layouts: none -> 3.72 us  [local(): pl.pallas_call(kernel, out_shape=(square, square, square, jax.ShapeDtypeS...]
  transfers between devices with their start and end apart: 3 -> 0, of which waited for: 3 -> 0; matrix products, arithmetic and copies ran while one was open for 4% -> 0% of each run, Pallas kernels for 0% -> 0%
where the time goes in v1:
time: 150 us; the launch traced here: 149 us
  Pallas kernels  117 us (78%)
  other arithmetic  25.6 us (17%)
  local copies, waits for them, and re-layouts  3.9 us (3%)
    pallas_call x1, Pallas kernels, local(): pl.pallas_call(kernel, out_shape=(square, square, square, jax.ShapeDtypeS...  117 us
    another operation x3, other arithmetic, local(): lower = jnp.linalg.cholesky(core)  12.4 us
    another operation x2, other arithmetic, local(): return jax.scipy.linalg.solve_triangular(lower, shifted.T, lower=True).T  10.5 us
    pallas_call x4, local copies, waits for them, and re-layouts, local(): pl.pallas_call(kernel, out_shape=(square, square, square, jax.ShapeDtypeS...  3.72 us

profile of v1, /device:TPU:1, one launch (start us, length us, event | category | flops | bytes accessed | tf_op | source)
XLA Modules:
  0.0 149.3 jit_solution(16396748858110595322)
XLA Ops:
  0.0 117.4 %gather_project_sketch.1 = (f32[128,128]{1,0:T(8,128)}, f32[128,128]{1,0:T(8,128)}, f32[128,128]{1,0:T(8,128)}, f32[1,128]{1,0:T(1,128)}, f32[128,128]{1,0:T(8,128)}) custom-call(bf16[512,1024]{1,0:T(8,128)(2,1)} %tok_h.1, bf16[512,4096]{1,0:T(8,128)(2,1)} %go_h.1, bf16[512,3584]{1,0:T(8,128)(2,1)} %gp_h.1, bf16[512,3584]{1,0:T(8,128)(2,1)} %up_h.1, ...), custom_call_target="tpu_custom_call" | custom-call | tf_op jit(solution)/shard_map/gather_project_sketch/pallas_call | solution.py:423
  117.4 1.5 select_reduce_fusion.1
  119.5 1.3 reduce_sum.19
  121.5 0.9 copy.10
  122.4 0.9 copy.9
  123.4 0.9 copy.12
  124.3 0.9 copy.11
  125.3 0.1 copy.13
  125.4 0.1 copy.14
  125.5 11.7 %cholesky.13 = f32[128,128]{1,0:T(8,128)S(1)} custom-call(f32[128,128]{1,0:T(8,128)S(1)} %fusion.3), custom_call_target="Cholesky" | custom-call | tf_op jit(solution)/shard_map/jit(cholesky)/cholesky | solution.py:447
  137.2 0.6 compare_reduce_fusion
  137.9 0.7 fusion
  138.6 9.8 %custom-call.7 = f32[1,128,128]{1,2,0:T(8,128)S(1)} custom-call(f32[1,128,128]{2,1,0:T(8,128)S(1)} %fusion), custom_call_target="InvertDiagBlocksLowerTriangular" | custom-call | tf_op jit(solution)/shard_map/jit(_solve_triangular)/triangular_solve | solution.py:449
  148.4 0.9 fusion.1
  (4 shorter events, 0.1 us)

commit v2 on v1

--- a/solution.py
+++ b/solution.py
@@ -39,10 +39,10 @@
 
 def kernel(
     tok_h, go_h, gp_h, up_h, dw_h, ip_h, op_h, tm_h,
-    y_o, a_o, gram_o, nr_o, om_o,
+    y_o, a_o, gram_o, nr_o, sq_o, om_o,
     w_s, g_s, gp_s, up_s, acc_s, m_s, tk_s, ip_s, op_s, tm_s,
     oacc_s, sb_s, pb_s, oa_s, xb_s, xr_s, ap_s, ar_s,
-    p32_s, pr_s, cs_s, cr_s, ns_s, nr_s,
+    p32_s, pr_s, cs_s, cr_s, ns_s, nr_s, gram_s,
     lsem, psend, precv, ssem, rsem, sbsend, sbrecv, xsend, xrecv, asend, arecv, tsend, trecv,
 ):
     d = lax.axis_index("dp")
@@ -241,7 +241,7 @@
             x = tm_s[pl.ds(pl.multiple_of(i * 1024, 1024), 1024), :]
             return total + tn(x, x)
 
-        gram_o[...] = lax.fori_loop(0, 16, part, jnp.zeros((128, 128), jnp.float32))
+        gram_s[...] = lax.fori_loop(0, 16, part, jnp.zeros((128, 128), jnp.float32))
 
     def at(step):
         w, k = divmod(step, 16)
@@ -396,7 +396,12 @@
     everyone(lambda k, dev: remote(ns_s, nr_s.at[me], tsend.at[2], trecv.at[2], dev))
     nr_s[me] = squares
     y_o[...] = sketch
-    a_o[...] = tn(wide, narrow.astype(jnp.float32), precision=lax.Precision.HIGHEST)
+    core = tn(wide, narrow.astype(jnp.float32), precision=lax.Precision.HIGHEST)
+    a_o[...] = 0.5 * (core + core.T)
+    gram_all = gram_s[...]
+    gram_o[...] = 0.5 * (gram_all + gram_all.T)
+    eye = lax.broadcasted_iota(jnp.int32, (128, 128), 0) == lax.broadcasted_iota(jnp.int32, (128, 128), 1)
+    sq_o[...] = jnp.sum(jnp.where(eye, gram_all, 0.0), axis=0, keepdims=True)
 
     for i, (r0, rn) in enumerate(sends):
         ref = w_s.at[0, pl.ds(r0, rn)]
@@ -415,16 +420,80 @@
     nr_o[...] = jnp.sum(nr_s[:, 0, :], axis=0, keepdims=True)
 
 
+def eliminate(groups):
+    groups = list(groups)
+    lane = lax.broadcasted_iota(jnp.int32, (8, 128), 1)
+    sub = lax.broadcasted_iota(jnp.int32, (8, 128), 0)
+
+    def wide(x):
+        return jnp.broadcast_to(x, (8, 128))
+
+    for g in range(16):
+        k0 = 8 * g
+        inside = (lane >= k0) & (lane < k0 + 8)
+        block = groups[g]
+        columns = [wide(block[:, k0 + b : k0 + b + 1]) for b in range(8)]
+        low = [[wide(columns[b][a : a + 1, :]) if b >= a else None for b in range(8)] for a in range(8)]
+        mult = [[None] * 8 for _ in range(8)]
+        inv = []
+        for a in range(8):
+            inv.append(1.0 / low[a][a])
+            for b in range(a + 1, 8):
+                mult[b][a] = low[a][b] * inv[a]
+            for b in range(a + 1, 8):
+                for e in range(b, 8):
+                    low[b][e] = low[b][e] - mult[b][a] * low[a][e]
+        rows = []
+        for a in range(8):
+            x = jnp.where(inside, jnp.where(lane == k0 + a, 1.0, 0.0), wide(block[a : a + 1, :]))
+            for b in range(a):
+                x = x - mult[a][b] * rows[b]
+            rows.append(x)
+        done = block
+        for a in range(8):
+            done = jnp.where(sub == a, rows[a] * lax.rsqrt(low[a][a]), done)
+        groups[g] = done
+        for h in range(g + 1, 16):
+            below = groups[h]
+            solved = []
+            for a in range(8):
+                x = wide(below[:, k0 + a : k0 + a + 1])
+                for b in range(a):
+                    x = x - mult[a][b] * solved[b]
+                solved.append(x)
+            x = jnp.where(inside, 0.0, below)
+            for a in range(8):
+                x = x - (solved[a] * inv[a]) * rows[a]
+            groups[h] = x
+    return groups
+
+
+def finish(y_ref, core_ref, gram_ref, nr_ref, sq_ref, om_ref, out_ref):
+    square_sum = jnp.sum(nr_ref[...], axis=1, keepdims=True)
+    omega_sq = jnp.sum(sq_ref[...], axis=1, keepdims=True)
+    shift = shift_scale * jnp.sqrt(square_sum / (omega_sq + tiny_value))
+    core = core_ref[...] + shift * gram_ref[...]
+    inverse = jnp.concatenate(eliminate([core[8 * g : 8 * g + 8, :] for g in range(16)]), axis=0)
+    under = lax.broadcasted_iota(jnp.int32, (128, 128), 1) <= lax.broadcasted_iota(jnp.int32, (128, 128), 0)
+    inverse = jnp.where(under, inverse, 0.0)
+    shifted = y_ref[...] + shift * om_ref[...]
+    out_ref[...] = lax.dot_general(
+        shifted, inverse, (((1,), (1,)), ((), ())),
+        precision=lax.Precision.HIGHEST, preferred_element_type=jnp.float32,
+    )
+
+
 def local(tokens, grad_out, gate_pre, up_value, down_weight, in_proj, out_proj, test_matrix):
     f32, bf16 = jnp.float32, jnp.bfloat16
     square = jax.ShapeDtypeStruct((128, 128), f32)
     vmem = pltpu.VMEM
     dma = pltpu.SemaphoreType.DMA
-    sketch, core_sketch, gram, squares, omega_own = pl.pallas_call(
+    row = jax.ShapeDtypeStruct((1, 128), f32)
+    sketch, core_sketch, gram, squares, omega_sq, omega_own = pl.pallas_call(
         kernel,
-        out_shape=(square, square, square, jax.ShapeDtypeStruct((1, 128), f32), square),
+        out_shape=(square, square, square, row, row, square),
         in_specs=[pl.BlockSpec(memory_space=pl.ANY)] * 8,
-        out_specs=(pl.BlockSpec(memory_space=vmem),) * 5,
+        out_specs=(pl.BlockSpec(memory_space=vmem),) * 6,
         scratch_shapes=[
             vmem((16, 1792, 256), bf16), vmem((1024, 4096), bf16), vmem((1024, 1792), bf16), vmem((1024, 1792), bf16),
             vmem((7, 1024, 256), f32), vmem((1024, 768), f32), vmem((512, 1024), bf16), vmem((128, 1024), bf16),
@@ -432,7 +501,7 @@
             vmem((8, 128, 128), f32), vmem((4, 128, 128), f32), vmem((4, 128, 128), f32), vmem((4, 128, 128), f32),
             vmem((4, 128, 128), f32), vmem((4, 128, 128), f32), vmem((4, 128, 128), f32), vmem((4, 128, 128), f32),
             vmem((128, 1, 128), f32), vmem((128, 1, 128), f32), vmem((1, 128), f32), vmem((128, 1, 128), f32),
-            vmem((1, 128), f32), vmem((128, 1, 128), f32),
+            vmem((1, 128), f32), vmem((128, 1, 128), f32), vmem((128, 128), f32),
             dma((9,)), dma((5,)), dma((5,)), dma((NSEND,)), dma((16, 4)), dma((4,)), dma((4,)), dma((4,)), dma((4,)),
             dma((4,)), dma((4,)), dma((3,)), dma((3,)),
         ],
@@ -441,12 +510,13 @@
         ),
         name="gather_project_sketch",
     )(tokens, grad_out, gate_pre, up_value, down_weight, in_proj, out_proj, test_matrix)
-    shift = shift_scale * jnp.sqrt(jnp.sum(squares) / (jnp.trace(gram) + tiny_value))
-    core = core_sketch + shift * gram
-    core = 0.5 * (core + core.T)
-    lower = jnp.linalg.cholesky(core)
-    shifted = sketch + shift * omega_own
-    return jax.scipy.linalg.solve_triangular(lower, shifted.T, lower=True).T
+    return pl.pallas_call(
+        finish,
+        out_shape=square,
+        in_specs=[pl.BlockSpec(memory_space=vmem)] * 6,
+        out_specs=pl.BlockSpec(memory_space=vmem),
+        name="factor",
+    )(sketch, core_sketch, gram, squares, omega_sq, omega_own)
 
 
 def solution(mesh):

time: 150 us -> 124 us (0.83)
  other arithmetic: 25.6 us -> 0 us
  Pallas kernels: 117 us -> 124 us
  local copies, waits for them, and re-layouts: 3.9 us -> 0 us
    another operation x5 -> x0, other arithmetic: 22.9 us -> none  [the longest x3 12.4 us: local(): lower = jnp.linalg.cholesky(core)]
    pallas_call x1 -> x2, Pallas kernels: 117 us -> 124 us  [the longest x1 117 us: local(): pl.pallas_call(kernel, out_shape=(square, square, square, row, row, squar...]
    pallas_call x4 -> x0, local copies, waits for them, and re-layouts: 3.72 us -> none  [local(): pl.pallas_call(kernel, out_shape=(square, square, square, jax.ShapeDtypeS...]
    reduce_sum x2 -> x0, other arithmetic: 2.74 us -> none  [the longest x1 1.46 us: local(): jnp.trace(gram) + tiny_value]
where the time goes in v2:
time: 124 us
  Pallas kernels  124 us (100%)
    pallas_call x1, Pallas kernels, local(): pl.pallas_call(kernel, out_shape=(square, square, square, row, row, squar...  117 us
    pallas_call x1, Pallas kernels, local(): pl.pallas_call(finish, out_shape=square, in_specs=[pl.BlockSpec(memory_sp...  6.31 us

profile of v2, /device:TPU:1, one launch (start us, length us, event | category | flops | bytes accessed | tf_op | source)
XLA Modules:
  0.0 123.7 jit_solution(5745120488889284473)
XLA Ops:
  0.0 117.4 %gather_project_sketch.1 = (f32[128,128]{1,0:T(8,128)}, f32[128,128]{1,0:T(8,128)}, f32[128,128]{1,0:T(8,128)}, f32[1,128]{1,0:T(1,128)}, f32[1,128]{1,0:T(1,128)}, /*index=5*/f32[128,128]{1,0:T(8,128)}) custom-call(bf16[512,1024]{1,0:T(8,128)(2,1)} %tok_h.1, bf16[512,4096]{1,0:T(8,128)(2,1)} %go_h.1, bf16[512,3584]{1,0:T(8,128)(2,1)} %gp_h.1, ...), custom_call_target="tpu_custom_call" | custom-call | tf_op jit(solution)/shard_map/gather_project_sketch/pallas_call | solution.py:492
  117.4 6.3 %factor.1 = f32[128,128]{1,0:T(8,128)} custom-call(f32[128,128]{1,0:T(8,128)} %get-tuple-element.11.y_ref, f32[128,128]{1,0:T(8,128)} %get-tuple-element.12.core_ref, f32[128,128]{1,0:T(8,128)} %get-tuple-element.13.gram_ref, f32[1,128]{1,0:T(1,128)} %get-tuple-element.14.nr_ref, f32[1,128]{1,0:T(1,128)} %get-tuple-element.15.sq_ref, ...), custom_call_target="tpu_custom_call" | custom-call | tf_op jit(solution)/shard_map/factor/pallas_call | solution.py:513

commit v3 on v2

--- a/solution.py
+++ b/solution.py
@@ -18,7 +18,7 @@
 SLOT = {home: k for k, home in enumerate(ORDER)}
 ROWS = {(0, 0): (0, 512), (0, 1): (512, 512), (1, 0): (1024, 384), (1, 1): (1408, 384)}
 UP, UM, VP, VM = 0, 1, 2, 3
-NSEND = 60
+NSEND = 68
 
 
 def table(k, values):
@@ -132,6 +132,20 @@
         ).start()
         sends.append((r0, rn))
 
+    def start_own(mine_first):
+        which = c if mine_first else 1 - c
+        there = pl.ds(pl.multiple_of(which * 128, 128), 128)
+        for k in range(2):
+            for dirn, dst, h in ((UP, (3, 0), k), (UM, (1, 0), 1 - k), (VP, (0, 3), k), (VM, (0, 1), 1 - k)):
+                r0, rn = ROWS[(0, h)]
+                rows = pl.ds(r0, rn)
+                src = dw_h.at[pl.ds(half + r0, rn)] if mine_first else w_s.at[0, rows, there]
+                remote(
+                    src, w_s.at[SLOT[dst], rows, there],
+                    ssem.at[len(sends)], rsem.at[SLOT[dst], h], dirs[dirn],
+                ).start()
+                sends.append((r0, rn // 2))
+
     def landed(home, w, h):
         r0, rn = ROWS[(w, h)]
         ref = w_s.at[SLOT[home], pl.ds(r0, rn)]
@@ -162,10 +176,10 @@
             send(VP, (0, 0), (0, 3), w, k)
             send(VM, (0, 0), (0, 1), w, 1 - k)
 
+    start_own(True)
+    partner_copies(0).wait_recv()
+    start_own(False)
     locals_(0).wait()
-    partner_copies(0).wait_recv()
-    own_u(0)
-    own_v(0)
     for i in range(5, 9):
         locals_(i).start()
     partner_copies(3).start()
@@ -215,33 +229,22 @@
         s = 1.0 / (1.0 + jnp.exp(-g))
         return up_s[rows, cols].astype(jnp.float32) * s * (1.0 + g * (1.0 - s))
 
-    def gate_first():
-        def tile(i, carry):
-            rows = pl.ds(pl.multiple_of(i * 128, 128), 128)
-            total = jnp.zeros((128, 128), jnp.float32)
-            for n in range(4):
-                gg = (acc_s[n, rows, :] * gate(rows, n)).astype(jnp.bfloat16)
-                total = total + nt(gg, op_s[:, n * 256 : (n + 1) * 256])
-            oacc_s[i] = total
-            return carry
-
-        lax.fori_loop(0, 8, tile, 0)
-
-    def gate_ahead():
-        def tile(i, carry):
-            rows = pl.ds(pl.multiple_of(i * 128, 128), 128)
-            for n in range(3):
-                m_s[rows, n * 256 : (n + 1) * 256] = gate(rows, n + 4)
-            return carry
-
-        lax.fori_loop(0, 8, tile, 0)
-
-    def gram():
-        def part(i, total):
-            x = tm_s[pl.ds(pl.multiple_of(i * 1024, 1024), 1024), :]
-            return total + tn(x, x)
-
-        gram_s[...] = lax.fori_loop(0, 16, part, jnp.zeros((128, 128), jnp.float32))
+    def gate_tile(i):
+        rows = pl.ds(pl.multiple_of(i * 128, 128), 128)
+        total = jnp.zeros((128, 128), jnp.float32)
+        for n in range(4):
+            gg = (acc_s[n, rows, :] * gate(rows, n)).astype(jnp.bfloat16)
+            total = total + nt(gg, op_s[:, n * 256 : (n + 1) * 256])
+        oacc_s[i] = total
+
+    def gate_ahead_tile(i):
+        rows = pl.ds(pl.multiple_of(i * 128, 128), 128)
+        for n in range(3):
+            m_s[rows, n * 256 : (n + 1) * 256] = gate(rows, n + 4)
+
+    def gram_part(i):
+        x = tm_s[pl.ds(pl.multiple_of(i * 2048, 2048), 2048), :]
+        gram_s[...] += tn(x, x)
 
     def at(step):
         w, k = divmod(step, 16)
@@ -272,22 +275,26 @@
             both((1, 2), w)
         if k == 15:
             both((2, 2), w)
-        if step == 20:
-            for i in range(5, 8):
+        if step == 1:
+            for i in range(5, 9):
                 locals_(i).wait()
             partner_copies(3).wait_recv()
             partner_copies(4).wait_recv()
-            gate_first()
-        if step == 23:
-            gate_ahead()
-        if step == 25:
-            locals_(8).wait()
-            gram()
+            gram_s[...] = jnp.zeros((128, 128), jnp.float32)
 
     def step_body(e, carry):
         for step in range(32):
-            if step in (3, 5, 6, 8, 10, 13, 14, 15, 19, 20, 21, 22, 23, 24, 25, 26, 29, 30, 31):
+            if step in (1, 3, 5, 6, 8, 10, 13, 14, 15, 19, 20, 21, 22, 23, 24, 25, 26, 29, 30, 31):
                 pl.when(e == step)(functools.partial(at, step))
+        @pl.when((e >= 2) & (e < 10))
+        def _():
+            gram_part(e - 2)
+            gate_ahead_tile(e - 2)
+
+        @pl.when((e >= 17) & (e < 25))
+        def _():
+            gate_tile(e - 17)
+
         w = lax.div(e, 16)
         k = lax.rem(e, 16)
         du = table(k, [h[0] for h in ORDER])
@@ -365,19 +372,15 @@
     everyone(lambda k, dev: remote(p32_s.at[k], pr_s.at[me], tsend.at[0], trecv.at[0], dev))
     pr_s[me] = p32_s[me]
 
-    def coeff_part(i, totals):
-        out = []
-        for b in range(8):
-            row = p32_s[i * 8 + b].astype(jnp.bfloat16)
-            rows = pl.ds(pl.multiple_of(i * 1024 + b * 128, 128), 128)
-            out.append(
-                totals[b]
-                + lax.dot_general(row, tm_s[rows, :], (((1,), (0,)), ((), ())), preferred_element_type=jnp.float32)
-            )
-        return tuple(out)
-
-    totals = lax.fori_loop(0, 16, coeff_part, tuple(jnp.zeros((1, 128), jnp.float32) for _ in range(8)))
-    coeff = ((totals[0] + totals[1]) + (totals[2] + totals[3])) + ((totals[4] + totals[5]) + (totals[6] + totals[7]))
+    across = tn(out, act).astype(jnp.bfloat16).astype(jnp.float32)
+    totals = [jnp.zeros((8, 128), jnp.float32) for _ in range(8)]
+    for i in range(128):
+        column = jnp.broadcast_to(across[:, i : i + 1], (128, 128))
+        product = column * tm_s[i * 128 : (i + 1) * 128, :].astype(jnp.float32)
+        for b in range(16):
+            totals[b % 8] = totals[b % 8] + product[8 * b : 8 * b + 8, :]
+    total = ((totals[0] + totals[1]) + (totals[2] + totals[3])) + ((totals[4] + totals[5]) + (totals[6] + totals[7]))
+    coeff = jnp.sum(total, axis=0, keepdims=True)
     cs_s[...] = coeff
     everyone(lambda k, dev: remote(cs_s, cr_s.at[me], tsend.at[1], trecv.at[1], dev))
     cr_s[me] = coeff

time: 124 us -> 117 us (0.944)
  Pallas kernels: 124 us -> 116 us
    pallas_call x1, Pallas kernels: 117 us -> 110 us  [local(): pl.pallas_call(kernel, out_shape=(square, square, square, row, row, squar...]
where the time goes in v3:
time: 117 us; the launch traced here: 116 us
  Pallas kernels  116 us (99%)
    pallas_call x1, Pallas kernels, local(): pl.pallas_call(kernel, out_shape=(square, square, square, row, row, squar...  110 us
    pallas_call x1, Pallas kernels, local(): pl.pallas_call(finish, out_shape=square, in_specs=[pl.BlockSpec(memory_sp...  6.31 us

profile of v3, /device:TPU:1, one launch (start us, length us, event | category | flops | bytes accessed | tf_op | source)
XLA Modules:
  0.0 116.4 jit_solution(14465406072920655967)
XLA Ops:
  0.0 110.1 %gather_project_sketch.1 = (f32[128,128]{1,0:T(8,128)}, f32[128,128]{1,0:T(8,128)}, f32[128,128]{1,0:T(8,128)}, f32[1,128]{1,0:T(1,128)}, f32[1,128]{1,0:T(1,128)}, /*index=5*/f32[128,128]{1,0:T(8,128)}) custom-call(bf16[512,1024]{1,0:T(8,128)(2,1)} %tok_h.1, bf16[512,4096]{1,0:T(8,128)(2,1)} %go_h.1, bf16[512,3584]{1,0:T(8,128)(2,1)} %gp_h.1, ...), custom_call_target="tpu_custom_call" | custom-call | tf_op jit(solution)/shard_map/gather_project_sketch/pallas_call | solution.py:495
  110.1 6.3 %factor.1 = f32[128,128]{1,0:T(8,128)} custom-call(f32[128,128]{1,0:T(8,128)} %get-tuple-element.11.y_ref, f32[128,128]{1,0:T(8,128)} %get-tuple-element.12.core_ref, f32[128,128]{1,0:T(8,128)} %get-tuple-element.13.gram_ref, f32[1,128]{1,0:T(1,128)} %get-tuple-element.14.nr_ref, f32[1,128]{1,0:T(1,128)} %get-tuple-element.15.sq_ref, ...), custom_call_target="tpu_custom_call" | custom-call | tf_op jit(solution)/shard_map/factor/pallas_call | solution.py:516

commit v4 on v3

--- a/solution.py
+++ b/solution.py
@@ -16,9 +16,14 @@
     (1, 3), (1, 1), (0, 2), (2, 3), (2, 1), (3, 2), (1, 2), (2, 2),
 ]
 SLOT = {home: k for k, home in enumerate(ORDER)}
-ROWS = {(0, 0): (0, 512), (0, 1): (512, 512), (1, 0): (1024, 384), (1, 1): (1408, 384)}
+TILES = [4, 3]
+BASE = [sum(TILES[:w]) for w in range(len(TILES))]
+LAST = len(TILES) - 1
+ROWS = {(w, h): (256 * BASE[w] + 128 * TILES[w] * h, 128 * TILES[w]) for w in range(LAST + 1) for h in range(2)}
+FIRST = 256 * TILES[0]
+REST = 1792 - FIRST
 UP, UM, VP, VM = 0, 1, 2, 3
-NSEND = 68
+NSEND = 30 * len(TILES) + 8
 
 
 def table(k, values):
@@ -29,6 +34,13 @@
     return total
 
 
+def packed(k, values):
+    code = [sum(v << (2 * j) for j, v in enumerate(values[i : i + 8])) for i in (0, 8)]
+    upper = (k >= 8).astype(jnp.int32)
+    word = code[0] + upper * (code[1] - code[0])
+    return lax.shift_right_arithmetic(word, 2 * (k - 8 * upper)) & 3
+
+
 def nt(a, b):
     return lax.dot_general(a, b, (((1,), (1,)), ((), ())), preferred_element_type=jnp.float32)
 
@@ -39,11 +51,11 @@
 
 def kernel(
     tok_h, go_h, gp_h, up_h, dw_h, ip_h, op_h, tm_h,
-    y_o, a_o, gram_o, nr_o, sq_o, om_o,
+    y_h, a_h, gram_h, nr_h, sq_h, om_h,
     w_s, g_s, gp_s, up_s, acc_s, m_s, tk_s, ip_s, op_s, tm_s,
     oacc_s, sb_s, pb_s, oa_s, xb_s, xr_s, ap_s, ar_s,
-    p32_s, pr_s, cs_s, cr_s, ns_s, nr_s, gram_s,
-    lsem, psend, precv, ssem, rsem, sbsend, sbrecv, xsend, xrecv, asend, arecv, tsend, trecv,
+    p32_s, pr_s, ns_s, nr_s, gram_s, y_o, a_o, gram_o, nr_o, sq_o, om_o,
+    lsem, psend, precv, ssem, rsem, sbsend, sbrecv, xsend, xrecv, asend, arecv, tsend, trecv, osem,
 ):
     d = lax.axis_index("dp")
     t = lax.axis_index("tensor")
@@ -79,9 +91,9 @@
 
     def locals_(i):
         if i == 0:
-            return local(0, dw_h.at[pl.ds(half, 1024)], w_s.at[0, pl.ds(0, 1024), lanes])
+            return local(0, dw_h.at[pl.ds(half, FIRST)], w_s.at[0, pl.ds(0, FIRST), lanes])
         if i == 1:
-            return local(1, dw_h.at[pl.ds(half + 1024, 768)], w_s.at[0, pl.ds(1024, 768), lanes])
+            return local(1, dw_h.at[pl.ds(half + FIRST, REST)], w_s.at[0, pl.ds(FIRST, REST), lanes])
         src, dst = [
             (go_h, g_s.at[mine]),
             (tok_h, tk_s),
@@ -97,7 +109,7 @@
         locals_(i).start()
 
     barrier = pltpu.get_barrier_semaphore()
-    greeted = [partner] + dirs + xdev[1:]
+    greeted = [partner] + dirs + [xdev[1], xdev[3]]
     for dev in greeted:
         pl.semaphore_signal(barrier, 1, device_id=dev, device_id_type=MESH)
     pl.semaphore_wait(barrier, len(greeted))
@@ -109,8 +121,8 @@
 
     def partner_copies(i):
         src, dst = [
-            lambda: (dw_h.at[pl.ds(other, 1024)], w_s.at[0, pl.ds(0, 1024), lanes]),
-            lambda: (dw_h.at[pl.ds(other + 1024, 768)], w_s.at[0, pl.ds(1024, 768), lanes]),
+            lambda: (dw_h.at[pl.ds(other, FIRST)], w_s.at[0, pl.ds(0, FIRST), lanes]),
+            lambda: (dw_h.at[pl.ds(other + FIRST, REST)], w_s.at[0, pl.ds(FIRST, REST), lanes]),
             lambda: (go_h, g_s.at[mine]),
             lambda: (gp_h.at[:, pl.ds(other, 1792)], gp_s.at[mine]),
             lambda: (up_h.at[:, pl.ds(other, 1792)], up_s.at[mine]),
@@ -200,8 +212,8 @@
     def act_copies(j):
         return remote(ap_s.at[j], ar_s.at[j], asend.at[j], arecv.at[j], xdev[j])
 
-    for j in (2, 1, 3):
-        act_copies(j).start()
+    act_copies(1).start()
+    act_copies(3).start()
 
     def first_events(w):
         event((3, 0), w, 0)
@@ -229,18 +241,18 @@
         s = 1.0 / (1.0 + jnp.exp(-g))
         return up_s[rows, cols].astype(jnp.float32) * s * (1.0 + g * (1.0 - s))
 
-    def gate_tile(i):
+    def gate_tile(w, i):
         rows = pl.ds(pl.multiple_of(i * 128, 128), 128)
-        total = jnp.zeros((128, 128), jnp.float32)
-        for n in range(4):
+        total = oacc_s[i] if w else jnp.zeros((128, 128), jnp.float32)
+        for n in range(BASE[w], BASE[w + 1]):
             gg = (acc_s[n, rows, :] * gate(rows, n)).astype(jnp.bfloat16)
             total = total + nt(gg, op_s[:, n * 256 : (n + 1) * 256])
         oacc_s[i] = total
 
     def gate_ahead_tile(i):
         rows = pl.ds(pl.multiple_of(i * 128, 128), 128)
-        for n in range(3):
-            m_s[rows, n * 256 : (n + 1) * 256] = gate(rows, n + 4)
+        for n in range(TILES[LAST]):
+            m_s[rows, n * 256 : (n + 1) * 256] = gate(rows, n + BASE[LAST])
 
     def gram_part(i):
         x = tm_s[pl.ds(pl.multiple_of(i * 2048, 2048), 2048), :]
@@ -248,8 +260,6 @@
 
     def at(step):
         w, k = divmod(step, 16)
-        if k == 0 and w == 1:
-            pass
         if k == 3:
             pair_events(0, w)
         if k == 5:
@@ -257,20 +267,21 @@
             if w == 0:
                 locals_(1).wait()
                 partner_copies(1).wait_recv()
-                own_u(1)
+            if w < LAST:
+                own_u(w + 1)
         if k == 6:
             pair_events(3, w)
         if k == 8:
             pair_events(1, w)
         if k == 10:
             pair_events(2, w)
-            if w == 0:
-                own_v(1)
+            if w < LAST:
+                own_v(w + 1)
             both((0, 2), w)
         if k == 13:
             both((3, 2), w)
-            if w == 0:
-                first_events(1)
+            if w < LAST:
+                first_events(w + 1)
         if k == 14:
             both((1, 2), w)
         if k == 15:
@@ -281,37 +292,43 @@
             partner_copies(3).wait_recv()
             partner_copies(4).wait_recv()
             gram_s[...] = jnp.zeros((128, 128), jnp.float32)
+            act_copies(1).wait_recv()
+            act_copies(2).start()
 
     def step_body(e, carry):
-        for step in range(32):
-            if step in (1, 3, 5, 6, 8, 10, 13, 14, 15, 19, 20, 21, 22, 23, 24, 25, 26, 29, 30, 31):
-                pl.when(e == step)(functools.partial(at, step))
+        def events(group):
+            for step in range(8 * group, 8 * group + 8):
+                if step == 1 or step % 16 in (3, 5, 6, 8, 10, 13, 14, 15):
+                    pl.when(e == step)(functools.partial(at, step))
+
+        for group in range(2 * len(TILES)):
+            pl.when(lax.div(e, 8) == group)(functools.partial(events, group))
         @pl.when((e >= 2) & (e < 10))
         def _():
             gram_part(e - 2)
             gate_ahead_tile(e - 2)
 
-        @pl.when((e >= 17) & (e < 25))
-        def _():
-            gate_tile(e - 17)
+        for wave in range(LAST):
+            begin = 16 * wave + 17
+            pl.when((e >= begin) & (e < begin + 8))(functools.partial(lambda wave, begin: gate_tile(wave, e - begin), wave, begin))
 
         w = lax.div(e, 16)
         k = lax.rem(e, 16)
-        du = table(k, [h[0] for h in ORDER])
-        dv = table(k, [h[1] for h in ORDER])
+        du = packed(k, [h[0] for h in ORDER])
+        dv = packed(k, [h[1] for h in ORDER])
         q = chip(lax.rem(u + du, 4), lax.rem(v + dv, 4))
         cols = pl.ds(pl.multiple_of(q * 256, 256), 256)
 
         def part(n, carry):
-            m = w * 4 + n
+            m = table(w, BASE) + n
             b = w_s[k, pl.ds(pl.multiple_of(m * 256, 256), 256), :]
             acc_s[m] += nt(g_s[:, cols], b)
             return carry
 
-        lax.fori_loop(0, 4 - w, part, 0)
+        lax.fori_loop(0, table(w, TILES), part, 0)
         return carry
 
-    lax.fori_loop(0, 32, step_body, 0)
+    lax.fori_loop(0, 16 * len(TILES), step_body, 0)
 
     def pb_copy(j):
         return remote(sb_s.at[j], pb_s.at[j], sbsend.at[j], sbrecv.at[j], partner)
@@ -326,15 +343,15 @@
             x_copies(j).start()
 
     def tail(i, carry):
-        j = table(lax.div(i, 2), [2, 1, 3, 0])
-        own = lax.rem(i, 2)
+        j = table(i, [2, 1, 3, 2, 1, 3, 0, 0])
+        own = table(i, [0, 0, 0, 1, 1, 1, 0, 1])
         core = own * c + (1 - own) * (1 - c)
         k = core * 4 + lax.rem(t + j, 4)
         rows = pl.ds(pl.multiple_of(k * 128, 128), 128)
         total = oacc_s[k]
-        for n in range(3):
-            gg = (acc_s[n + 4, rows, :] * m_s[rows, n * 256 : (n + 1) * 256]).astype(jnp.bfloat16)
-            total = total + nt(gg, op_s[:, (n + 4) * 256 : (n + 5) * 256])
+        for n in range(TILES[LAST]):
+            gg = (acc_s[n + BASE[LAST], rows, :] * m_s[rows, n * 256 : (n + 1) * 256]).astype(jnp.bfloat16)
+            total = total + nt(gg, op_s[:, (n + BASE[LAST]) * 256 : (n + BASE[LAST] + 1) * 256])
 
         @pl.when(own == 0)
         def _():
@@ -345,13 +362,13 @@
         def _():
             oa_s[j] = total
 
-        for step, jj in ((3, 2), (5, 1), (7, 3)):
+        for step, jj in ((3, 2), (4, 1), (5, 3)):
             pl.when(i == step)(functools.partial(combine, jj))
         return carry
 
     lax.fori_loop(0, 8, tail, 0)
     combine(0)
-    for j in (1, 2, 3):
+    for j in (2, 3):
         act_copies(j).wait_recv()
     act = (ap_s[0] + ar_s[1] + ar_s[2] + ar_s[3]).astype(jnp.bfloat16)
     for j in (1, 2, 3):
@@ -359,7 +376,7 @@
     out = (xb_s[0] + xr_s[1] + xr_s[2] + xr_s[3]).astype(jnp.bfloat16)
 
     proj = tn(act, out).astype(jnp.bfloat16).astype(jnp.float32)
-    p32_s[...] = proj[:, None, :]
+    p32_s[:, 0, :] = proj
 
     def everyone(copy_to):
         def body(r, carry):
@@ -368,9 +385,6 @@
             return carry
 
         lax.fori_loop(1, 128, body, 0, unroll=4)
-
-    everyone(lambda k, dev: remote(p32_s.at[k], pr_s.at[me], tsend.at[0], trecv.at[0], dev))
-    pr_s[me] = p32_s[me]
 
     across = tn(out, act).astype(jnp.bfloat16).astype(jnp.float32)
     totals = [jnp.zeros((8, 128), jnp.float32) for _ in range(8)]
@@ -381,22 +395,21 @@
             totals[b % 8] = totals[b % 8] + product[8 * b : 8 * b + 8, :]
     total = ((totals[0] + totals[1]) + (totals[2] + totals[3])) + ((totals[4] + totals[5]) + (totals[6] + totals[7]))
     coeff = jnp.sum(total, axis=0, keepdims=True)
-    cs_s[...] = coeff
-    everyone(lambda k, dev: remote(cs_s, cr_s.at[me], tsend.at[1], trecv.at[1], dev))
-    cr_s[me] = coeff
+    p32_s[:, 1, :] = jnp.broadcast_to(coeff, (128, 128))
+    everyone(lambda k, dev: remote(p32_s.at[k], pr_s.at[me], tsend.at[0], trecv.at[0], dev))
+    pr_s[me] = p32_s[me]
     om_o[...] = tm_s[pl.ds(pl.multiple_of(me * 128, 128), 128), :].astype(jnp.float32)
 
     def drain(i, ref):
         return remote(ref.at[pl.ds(0, 127)], ref.at[pl.ds(0, 127)], tsend.at[i], trecv.at[i], partner)
 
     drain(0, pr_s).wait_recv()
-    drain(1, cr_s).wait_recv()
-    wide = cr_s[:, 0, :]
+    wide = pr_s[:, 1, :]
     narrow = wide.astype(jnp.bfloat16)
     sketch = tn(pr_s[:, 0, :].astype(jnp.bfloat16), narrow)
     squares = jnp.sum(sketch * sketch, axis=0, keepdims=True)
     ns_s[...] = squares
-    everyone(lambda k, dev: remote(ns_s, nr_s.at[me], tsend.at[2], trecv.at[2], dev))
+    everyone(lambda k, dev: remote(ns_s, nr_s.at[me], tsend.at[1], trecv.at[1], dev))
     nr_s[me] = squares
     y_o[...] = sketch
     core = tn(wide, narrow.astype(jnp.float32), precision=lax.Precision.HIGHEST)
@@ -405,6 +418,13 @@
     gram_o[...] = 0.5 * (gram_all + gram_all.T)
     eye = lax.broadcasted_iota(jnp.int32, (128, 128), 0) == lax.broadcasted_iota(jnp.int32, (128, 128), 1)
     sq_o[...] = jnp.sum(jnp.where(eye, gram_all, 0.0), axis=0, keepdims=True)
+
+    def leave(i):
+        src, dst = [(y_o, y_h), (a_o, a_h), (gram_o, gram_h), (sq_o, sq_h), (om_o, om_h), (nr_o, nr_h)][i]
+        return pltpu.make_async_copy(src, dst, osem.at[i])
+
+    for i in range(5):
+        leave(i).start()
 
     for i, (r0, rn) in enumerate(sends):
         ref = w_s.at[0, pl.ds(r0, rn)]
@@ -417,10 +437,12 @@
     for j in range(4):
         pb_copy(j).wait_send()
     drain(0, pr_s).wait_send()
-    drain(1, cr_s).wait_send()
-    drain(2, nr_s).wait_recv()
-    drain(2, nr_s).wait_send()
+    drain(1, nr_s).wait_recv()
+    drain(1, nr_s).wait_send()
     nr_o[...] = jnp.sum(nr_s[:, 0, :], axis=0, keepdims=True)
+    leave(5).start()
+    for i in range(6):
+        leave(i).wait()
 
 
 def eliminate(groups):
@@ -452,21 +474,19 @@
             for b in range(a):
                 x = x - mult[a][b] * rows[b]
             rows.append(x)
+        scaled = [rows[a] * inv[a] for a in range(8)]
         done = block
         for a in range(8):
             done = jnp.where(sub == a, rows[a] * lax.rsqrt(low[a][a]), done)
         groups[g] = done
         for h in range(g + 1, 16):
             below = groups[h]
-            solved = []
-            for a in range(8):
-                x = wide(below[:, k0 + a : k0 + a + 1])
-                for b in range(a):
-                    x = x - mult[a][b] * solved[b]
-                solved.append(x)
+            solved = [wide(below[:, k0 + a : k0 + a + 1]) for a in range(8)]
             x = jnp.where(inside, 0.0, below)
             for a in range(8):
-                x = x - (solved[a] * inv[a]) * rows[a]
+                for b in range(a + 1, 8):
+                    solved[b] = solved[b] - mult[b][a] * solved[a]
+                x = x - solved[a] * scaled[a]
             groups[h] = x
     return groups
 
@@ -496,17 +516,17 @@
         kernel,
         out_shape=(square, square, square, row, row, square),
         in_specs=[pl.BlockSpec(memory_space=pl.ANY)] * 8,
-        out_specs=(pl.BlockSpec(memory_space=vmem),) * 6,
+        out_specs=(pl.BlockSpec(memory_space=pl.ANY),) * 6,
         scratch_shapes=[
             vmem((16, 1792, 256), bf16), vmem((1024, 4096), bf16), vmem((1024, 1792), bf16), vmem((1024, 1792), bf16),
-            vmem((7, 1024, 256), f32), vmem((1024, 768), f32), vmem((512, 1024), bf16), vmem((128, 1024), bf16),
+            vmem((7, 1024, 256), f32), vmem((1024, 256 * TILES[LAST]), f32), vmem((512, 1024), bf16), vmem((128, 1024), bf16),
             vmem((128, 1792), bf16), vmem((16384, 128), bf16),
             vmem((8, 128, 128), f32), vmem((4, 128, 128), f32), vmem((4, 128, 128), f32), vmem((4, 128, 128), f32),
             vmem((4, 128, 128), f32), vmem((4, 128, 128), f32), vmem((4, 128, 128), f32), vmem((4, 128, 128), f32),
-            vmem((128, 1, 128), f32), vmem((128, 1, 128), f32), vmem((1, 128), f32), vmem((128, 1, 128), f32),
-            vmem((1, 128), f32), vmem((128, 1, 128), f32), vmem((128, 128), f32),
-            dma((9,)), dma((5,)), dma((5,)), dma((NSEND,)), dma((16, 4)), dma((4,)), dma((4,)), dma((4,)), dma((4,)),
-            dma((4,)), dma((4,)), dma((3,)), dma((3,)),
+            vmem((128, 2, 128), f32), vmem((128, 2, 128), f32), vmem((1, 128), f32), vmem((128, 1, 128), f32), vmem((128, 128), f32),
+            vmem((128, 128), f32), vmem((128, 128), f32), vmem((128, 128), f32), vmem((1, 128), f32), vmem((1, 128), f32), vmem((128, 128), f32),
+            dma((9,)), dma((5,)), dma((5,)), dma((NSEND,)), dma((16, 2 * len(TILES))), dma((4,)), dma((4,)), dma((4,)), dma((4,)),
+            dma((4,)), dma((4,)), dma((2,)), dma((2,)), dma((6,)),
         ],
         compiler_params=pltpu.CompilerParams(
             collective_id=1, has_side_effects=True, vmem_limit_bytes=60 * 1024 * 1024

time: 117 us -> 114 us (0.974)
  Pallas kernels: 116 us -> 114 us
    pallas_call x1, Pallas kernels: 110 us -> 108 us  [local(): pl.pallas_call(kernel, out_shape=(square, square, square, row, row, squar...]
where the time goes in v4:
time: 114 us
  Pallas kernels  114 us (100%)
    pallas_call x1, Pallas kernels, local(): pl.pallas_call(kernel, out_shape=(square, square, square, row, row, squar...  108 us
    pallas_call x1, Pallas kernels, local(): pl.pallas_call(finish, out_shape=square, in_specs=[pl.BlockSpec(memory_sp...  6.11 us

profile of v4, /device:TPU:1, one launch (start us, length us, event | category | flops | bytes accessed | tf_op | source)
XLA Modules:
  0.0 114.2 jit_solution(9540144521672975202)
XLA Ops:
  0.0 108.1 %gather_project_sketch.1 = (f32[128,128]{1,0:T(8,128)}, f32[128,128]{1,0:T(8,128)}, f32[128,128]{1,0:T(8,128)}, f32[1,128]{1,0:T(1,128)}, f32[1,128]{1,0:T(1,128)}, /*index=5*/f32[128,128]{1,0:T(8,128)}) custom-call(bf16[512,1024]{1,0:T(8,128)(2,1)} %tok_h.1, bf16[512,4096]{1,0:T(8,128)(2,1)} %go_h.1, bf16[512,3584]{1,0:T(8,128)(2,1)} %gp_h.1, ...), custom_call_target="tpu_custom_call" | custom-call | tf_op jit(solution)/shard_map/gather_project_sketch/pallas_call | solution.py:515
  108.1 6.1 %factor.1 = f32[128,128]{1,0:T(8,128)} custom-call(f32[128,128]{1,0:T(8,128)} %get-tuple-element.11.y_ref, f32[128,128]{1,0:T(8,128)} %get-tuple-element.12.core_ref, f32[128,128]{1,0:T(8,128)} %get-tuple-element.13.gram_ref, f32[1,128]{1,0:T(1,128)} %get-tuple-element.14.nr_ref, f32[1,128]{1,0:T(1,128)} %get-tuple-element.15.sq_ref, ...), custom_call_target="tpu_custom_call" | custom-call | tf_op jit(solution)/shard_map/factor/pallas_call | solution.py:536

commit v5 on v4

--- a/solution.py
+++ b/solution.py
@@ -380,21 +380,27 @@
 
     def everyone(copy_to):
         def body(r, carry):
-            k = lax.rem(me + r, 128)
-            copy_to(k, (lax.div(k, 4), lax.rem(k, 4))).start()
+            k = (me + r) & 127
+            copy_to(k, (lax.shift_right_arithmetic(k, 2), k & 3)).start()
             return carry
 
         lax.fori_loop(1, 128, body, 0, unroll=4)
 
     across = tn(out, act).astype(jnp.bfloat16).astype(jnp.float32)
     totals = [jnp.zeros((8, 128), jnp.float32) for _ in range(8)]
-    for i in range(128):
+    parts = [jnp.zeros((1, 128), jnp.float32) for _ in range(4)]
+    for i in range(88, 128):
+        row = proj[i : i + 1, :].astype(jnp.bfloat16)
+        parts[i % 4] = parts[i % 4] + lax.dot_general(
+            row, tm_s[i * 128 : (i + 1) * 128, :], (((1,), (0,)), ((), ())), preferred_element_type=jnp.float32
+        )
+    for i in range(88):
         column = jnp.broadcast_to(across[:, i : i + 1], (128, 128))
         product = column * tm_s[i * 128 : (i + 1) * 128, :].astype(jnp.float32)
         for b in range(16):
             totals[b % 8] = totals[b % 8] + product[8 * b : 8 * b + 8, :]
     total = ((totals[0] + totals[1]) + (totals[2] + totals[3])) + ((totals[4] + totals[5]) + (totals[6] + totals[7]))
-    coeff = jnp.sum(total, axis=0, keepdims=True)
+    coeff = jnp.sum(total, axis=0, keepdims=True) + ((parts[0] + parts[1]) + (parts[2] + parts[3]))
     p32_s[:, 1, :] = jnp.broadcast_to(coeff, (128, 128))
     everyone(lambda k, dev: remote(p32_s.at[k], pr_s.at[me], tsend.at[0], trecv.at[0], dev))
     pr_s[me] = p32_s[me]

time: 114 us -> 114 us (level)
  no operation moved by 1% of the time
where the time goes in v5:
time: 114 us
  Pallas kernels  114 us (100%)
    pallas_call x1, Pallas kernels, local(): pl.pallas_call(kernel, out_shape=(square, square, square, row, row, squar...  108 us
    pallas_call x1, Pallas kernels, local(): pl.pallas_call(finish, out_shape=square, in_specs=[pl.BlockSpec(memory_sp...  6.11 us

profile of v5, /device:TPU:1, one launch (start us, length us, event | category | flops | bytes accessed | tf_op | source)
XLA Modules:
  0.0 113.8 jit_solution(8305348197073311180)
XLA Ops:
  0.0 107.7 %gather_project_sketch.1 = (f32[128,128]{1,0:T(8,128)}, f32[128,128]{1,0:T(8,128)}, f32[128,128]{1,0:T(8,128)}, f32[1,128]{1,0:T(1,128)}, f32[1,128]{1,0:T(1,128)}, /*index=5*/f32[128,128]{1,0:T(8,128)}) custom-call(bf16[512,1024]{1,0:T(8,128)(2,1)} %tok_h.1, bf16[512,4096]{1,0:T(8,128)(2,1)} %go_h.1, bf16[512,3584]{1,0:T(8,128)(2,1)} %gp_h.1, ...), custom_call_target="tpu_custom_call" | custom-call | tf_op jit(solution)/shard_map/gather_project_sketch/pallas_call | solution.py:521
  107.7 6.1 %factor.1 = f32[128,128]{1,0:T(8,128)} custom-call(f32[128,128]{1,0:T(8,128)} %get-tuple-element.11.y_ref, f32[128,128]{1,0:T(8,128)} %get-tuple-element.12.core_ref, f32[128,128]{1,0:T(8,128)} %get-tuple-element.13.gram_ref, f32[1,128]{1,0:T(1,128)} %get-tuple-element.14.nr_ref, f32[1,128]{1,0:T(1,128)} %get-tuple-element.15.sq_ref, ...), custom_call_target="tpu_custom_call" | custom-call | tf_op jit(solution)/shard_map/factor/pallas_call | solution.py:542

commit v6 on v5

--- a/solution.py
+++ b/solution.py
@@ -389,12 +389,12 @@
     across = tn(out, act).astype(jnp.bfloat16).astype(jnp.float32)
     totals = [jnp.zeros((8, 128), jnp.float32) for _ in range(8)]
     parts = [jnp.zeros((1, 128), jnp.float32) for _ in range(4)]
-    for i in range(88, 128):
+    for i in range(72, 128):
         row = proj[i : i + 1, :].astype(jnp.bfloat16)
         parts[i % 4] = parts[i % 4] + lax.dot_general(
             row, tm_s[i * 128 : (i + 1) * 128, :], (((1,), (0,)), ((), ())), preferred_element_type=jnp.float32
         )
-    for i in range(88):
+    for i in range(72):
         column = jnp.broadcast_to(across[:, i : i + 1], (128, 128))
         product = column * tm_s[i * 128 : (i + 1) * 128, :].astype(jnp.float32)
         for b in range(16):

time: 114 us -> 114 us (level)
  no operation moved by 1% of the time
where the time goes in v6:
time: 114 us
  Pallas kernels  114 us (100%)
    pallas_call x1, Pallas kernels, local(): pl.pallas_call(kernel, out_shape=(square, square, square, row, row, squar...  108 us
    pallas_call x1, Pallas kernels, local(): pl.pallas_call(finish, out_shape=square, in_specs=[pl.BlockSpec(memory_sp...  6.11 us

profile of v6, /device:TPU:1, one launch (start us, length us, event | category | flops | bytes accessed | tf_op | source)
XLA Modules:
  0.0 113.7 jit_solution(12962302999179551615)
XLA Ops:
  0.0 107.6 %gather_project_sketch.1 = (f32[128,128]{1,0:T(8,128)}, f32[128,128]{1,0:T(8,128)}, f32[128,128]{1,0:T(8,128)}, f32[1,128]{1,0:T(1,128)}, f32[1,128]{1,0:T(1,128)}, /*index=5*/f32[128,128]{1,0:T(8,128)}) custom-call(bf16[512,1024]{1,0:T(8,128)(2,1)} %tok_h.1, bf16[512,4096]{1,0:T(8,128)(2,1)} %go_h.1, bf16[512,3584]{1,0:T(8,128)(2,1)} %gp_h.1, ...), custom_call_target="tpu_custom_call" | custom-call | tf_op jit(solution)/shard_map/gather_project_sketch/pallas_call | solution.py:521
  107.6 6.1 %factor.1 = f32[128,128]{1,0:T(8,128)} custom-call(f32[128,128]{1,0:T(8,128)} %get-tuple-element.11.y_ref, f32[128,128]{1,0:T(8,128)} %get-tuple-element.12.core_ref, f32[128,128]{1,0:T(8,128)} %get-tuple-element.13.gram_ref, f32[1,128]{1,0:T(1,128)} %get-tuple-element.14.nr_ref, f32[1,128]{1,0:T(1,128)} %get-tuple-element.15.sq_ref, ...), custom_call_target="tpu_custom_call" | custom-call | tf_op jit(solution)/shard_map/factor/pallas_call | solution.py:542
